TPU v7x, 32 devices: a whole 2x2x4 slice. The times are simulated.
32 devices in a mesh: seq: 4 (over y, x), tp: 8 (over z, core).
Axes of the slice: x: 2, y: 2, z: 4, core: 2. Of those that a mesh axis runs over, the one named last changes fastest.
Arguments:
- activations: bfloat16 [1024, 8192], P('seq', 'tp'), may hold values from -36 to 36
- norm_gain: bfloat16 [8192], P('tp'), may hold values from 0.099609375 to 1.8984375
- in_proj: bfloat16 [8192, 3, 4096], P(None, None, 'tp'), may hold values from -0.0625 to 0.0625
- short_taps: float32 [3, 3, 4096], P(None, None, 'tp'), may hold values from -3.5 to 3.5
- medium_taps: float32 [256, 128], P('tp'), may hold values from -0.5 to 0.5
- cotangent: bfloat16 [1024, 4096], P('seq', 'tp'), may hold values from -1.1953125 to 1.1953125
Outputs:
- mixer_out: bfloat16 [1024, 4096], P('seq', 'tp')
- grad_input: bfloat16 [1024, 8192], P('seq', 'tp')
- grad_proj: bfloat16 [8192, 3, 4096], P('seq', None, 'tp')
All inputs are finite; a program needn't handle non-finite values.
Results may differ from a plain program's by a relative error of at most 0.02.
Values may be sent and summed in bfloat16 or wider, within the bound.
No kernel may reach another device: no remote copies, remote signals or barrier semaphores. Data moves between devices by JAX's collectives and lax.ppermute only.
A program may use at most 192 MiB of HBM per device.

v0:
```python
import jax
import jax.numpy as jnp
from jax import lax
from jax.sharding import PartitionSpec as P

GROUP = 16
LS = 3
LM = 128
norm_eps = 1e-06


def shifted(block, axis, distance):
    devices = range(lax.axis_size(axis))
    route = [(i - distance, i) for i in devices if i - distance in devices]
    return lax.ppermute(block, axis, route)


def forward_short(source, taps, offset, length):
    total = jnp.zeros((length,) + source.shape[1:], jnp.float32)
    for index in range(LS):
        total = total + taps[index] * source[offset - index : offset - index + length].astype(
            jnp.float32
        )
    return total


def backward_short(source, taps, length):
    total = jnp.zeros((length,) + source.shape[1:], jnp.float32)
    for index in range(LS):
        total = total + taps[index] * source[index : index + length].astype(jnp.float32)
    return total


def band_matrix(tap_rows, out_len, in_len, lead, sign):
    offsets = lead + sign * (
        lax.broadcasted_iota(jnp.int32, (out_len, in_len), 0)
        - lax.broadcasted_iota(jnp.int32, (out_len, in_len), 1)
    )
    inside = (offsets >= 0) & (offsets < LM)
    picked = jnp.take(tap_rows, jnp.clip(offsets, 0, LM - 1), axis=1)
    return jnp.where(inside[None], picked, 0.0)


def grouped_apply(band, source):
    groups_here = band.shape[0]
    shaped = source.astype(jnp.float32).reshape(source.shape[0], groups_here, GROUP)
    result = jnp.einsum("gts,sgc->tgc", band, shaped, precision=lax.Precision.HIGHEST)
    return result.reshape(band.shape[1], groups_here * GROUP)


def per_device(activations, norm_gain, in_proj, short_taps, medium_taps, cotangent):
    act_full, gain_full = (
        lax.all_gather(activations, "tp", axis=1, tiled=True),
        lax.all_gather(norm_gain, "tp", axis=0, tiled=True),
    )
    tok_rows = act_full.shape[0]
    width = act_full.shape[1]
    local_ch = in_proj.shape[2]
    edge_rows = LM + LS - 2
    head_rows = LS - 1
    act_float = act_full.astype(jnp.float32)
    inv_rms = lax.rsqrt(jnp.mean(act_float * act_float, axis=1, keepdims=True) + norm_eps)
    gain_float = gain_full.astype(jnp.float32)
    normed = (act_float * inv_rms * gain_float).astype(jnp.bfloat16)
    weight = in_proj.reshape(width, 3 * local_ch)
    projected = (
        jnp.dot(normed, weight, preferred_element_type=jnp.float32)
        .astype(jnp.bfloat16)
        .reshape(tok_rows, 3, local_ch)
    )
    kv_tail = projected[tok_rows - edge_rows :, 1:, :].reshape(edge_rows, 2 * local_ch)
    q_tail = projected[tok_rows - head_rows :, 0, :].reshape(head_rows // 2, 2 * local_ch)
    received = shifted(jnp.concatenate([kv_tail, q_tail], 0), "seq", 1)
    kv_ext = jnp.concatenate(
        [received[:edge_rows].reshape(edge_rows, 2, local_ch), projected[:, 1:, :]], 0
    )
    q_ext = jnp.concatenate(
        [received[edge_rows:].reshape(head_rows, local_ch), projected[:, 0, :]], 0
    )
    span = tok_rows + LM - 1
    kv_feat = forward_short(kv_ext, short_taps[:, 1:, :], head_rows, span).astype(jnp.bfloat16)
    q_feat = forward_short(q_ext, short_taps[:, 0, :], head_rows, tok_rows).astype(jnp.bfloat16)
    gated = (kv_feat[:, 0].astype(jnp.float32) * kv_feat[:, 1].astype(jnp.float32)).astype(
        jnp.bfloat16
    )
    band_forward = band_matrix(medium_taps, tok_rows, span, LM - 1, 1)
    filtered = grouped_apply(band_forward, gated)
    mixer_out = (q_feat.astype(jnp.float32) * filtered).astype(jnp.bfloat16)
    grad_out = cotangent.astype(jnp.float32)
    grad_filtered = (grad_out * q_feat.astype(jnp.float32)).astype(jnp.bfloat16)
    grad_q = (grad_out * filtered).astype(jnp.bfloat16)
    kv_own = kv_feat[LM - 1 :]
    front = jnp.concatenate([grad_q[:head_rows, None, :], kv_own[:head_rows]], 1)
    outgoing = jnp.concatenate(
        [grad_filtered[:edge_rows], front.reshape(3 * head_rows, local_ch)], 0
    )
    returned = shifted(outgoing, "seq", -1)
    filt_ext = jnp.concatenate([grad_filtered, returned[:edge_rows]], 0)
    front_next = returned[edge_rows:].reshape(head_rows, 3, local_ch)
    reach = tok_rows + head_rows
    band_backward = band_matrix(medium_taps, reach, tok_rows + edge_rows, 0, -1)
    grad_gated = grouped_apply(band_backward, filt_ext)
    kv_reach = jnp.concatenate([kv_own, front_next[:, 1:, :]], 0)
    q_reach = jnp.concatenate([grad_q, front_next[:, 0, :]], 0)
    grad_k = (grad_gated * kv_reach[:, 1].astype(jnp.float32)).astype(jnp.bfloat16)
    grad_v = (grad_gated * kv_reach[:, 0].astype(jnp.float32)).astype(jnp.bfloat16)
    grad_feat = jnp.stack([q_reach, grad_k, grad_v], 1)
    grad_pre = (
        backward_short(grad_feat, short_taps, tok_rows)
        .astype(jnp.bfloat16)
        .reshape(tok_rows, 3 * local_ch)
    )
    partial_grad = lax.dot_general(
        grad_pre, weight, (((1,), (1,)), ((), ())), preferred_element_type=jnp.float32
    )
    tp_count = lax.axis_size("tp")
    own_width = width // tp_count
    own_scaled = activations.astype(jnp.float32) * inv_rms
    own_gain = norm_gain.astype(jnp.float32)
    whole_grad = lax.psum(partial_grad.astype(jnp.bfloat16), "tp").astype(jnp.float32)
    stat = jnp.mean(gain_float * whole_grad * act_float, axis=1, keepdims=True) * inv_rms
    grad_slice = lax.dynamic_slice_in_dim(
        whole_grad, lax.axis_index("tp") * own_width, own_width, 1
    )
    grad_scaled = own_gain * grad_slice
    grad_input = (inv_rms * (grad_scaled - own_scaled * stat)).astype(jnp.bfloat16)
    row_share = width // lax.axis_size("seq")
    norm_cols = lax.all_to_all(normed, "seq", split_axis=1, concat_axis=0, tiled=True)
    empty = jnp.zeros((row_share, 3 * local_ch), jnp.float32)
    total = empty
    piece = lax.all_gather(grad_pre, "seq", axis=0, tiled=True)
    blocks = piece.shape[0] // tok_rows
    for block in range(blocks):
        rows = lax.dynamic_slice_in_dim(norm_cols, block * tok_rows, tok_rows, 0)
        product = lax.dot_general(
            rows,
            piece[block * tok_rows : (block + 1) * tok_rows],
            (((0,), (0,)), ((), ())),
            preferred_element_type=jnp.float32,
        ).astype(jnp.bfloat16)
        product = lax.optimization_barrier(product)
        total = total + product.astype(jnp.float32)
    grad_proj = total.reshape(row_share, 3, local_ch).astype(jnp.bfloat16)
    return (mixer_out, grad_input, grad_proj)


def solution(mesh):
    return jax.shard_map(
        per_device,
        mesh=mesh,
        in_specs=(
            P("seq", "tp"),
            P("tp"),
            P(None, None, "tp"),
            P(None, None, "tp"),
            P("tp", None),
            P("seq", "tp"),
        ),
        out_specs=(P("seq", "tp"), P("seq", "tp"), P("seq", None, "tp")),
        check_vma=False,
    )
```

profile of v0, /device:TPU:0, one launch (start us, length us, event | category | flops | bytes accessed | tf_op | source)
XLA Modules:
  0.0 788.1 jit_solution(5932457810425270629)
XLA Ops:
  7.2 0.7 all-gather.3.cloned.1.call-update
  7.9 14.6 %all_gather.10 = bf16[8192]{0:T(1024)(128)(2,1)S(1)} all-gather(bf16[1024]{0:T(1024)(128)(2,1)} %param.7), channel_id=1, replica_groups=mesh['seq'=4,'tp'=8] {'tp'}, dimensions={0}, use_global_device_ids=true | all-gather | bytes 18432 | tf_op jit(solution)/shard_map/all_gather | solution.py:54
  22.6 33.6 %copy.88 = bf16[8192,3,512]{0,2,1:T(8,128)(2,1)} copy(bf16[8192,3,512]{2,0,1:T(8,128)(2,1)} %param.8) | data formatting | bytes 50331648 | tf_op args[2]
  56.2 0.5 reshape.180
  56.7 0.2 compare_select_fusion
  56.9 0.5 reshape.188
  57.5 1.7 all-gather.3.cloned.1.call-done
  59.2 3.3 fusion.13
  62.5 0.2 copy-done
  62.7 3.2 fusion.15
  65.9 12.8 %convolution_convert_fusion.4 = bf16[256,1536]{1,0:T(8,128)(2,1)S(1)} fusion(bf16[256,8192]{1,0:T(8,128)(2,1)} %fusion.15, bf16[8192,1536]{0,1:T(8,128)(2,1)} %bitcast.91), kind=kOutput, calls=%fused_computation.33 | convolution fusion | flops 6442844160 | bytes 30146560 | tf_op jit(solution)/shard_map/dot_general | solution.py:67
  78.7 0.3 copy.89
  79.0 0.2 slice.177
  79.2 0.1 slice.178
  79.3 0.2 copy.91
  79.5 0.1 copy.90
  79.7 3.8 collective-permute-start
  83.5 0.2 fusion.43
  83.8 179.7 %gather_fusion = f32[98048,32]{1,0:T(8,128)} fusion(f32[32,128]{0,1:T(8,128)S(1)} %copy.94, s32[98304]{0:T(1024)S(1)} %pad_clamp_fusion.1), kind=kCustom, calls=%fused_computation | custom fusion | bytes 25492480 | tf_op jit(solution)/shard_map/jit(_take)/gather | solution.py:40
  263.5 31.0 %copy.95 = f32[98048,32]{0,1:T(8,128)} copy(f32[98048,32]{1,0:T(8,128)} %gather_fusion) | data formatting | bytes 25100288 | tf_op jit(solution)/shard_map/jit(_take)/gather | solution.py:40
  294.5 18.2 %reshape.183 = f32[256,383,32]{1,0,2:T(8,128)} reshape(f32[98048,32]{0,1:T(8,128)} %copy.95) | data formatting | bytes 25100288 | tf_op jit(solution)/shard_map/jit(_take)/gather | solution.py:40
  312.7 0.1 copy.96
  312.9 0.2 copy.110
  313.1 1.7 add_convert_fusion.2
  314.9 0.1 slice.192
  315.1 0.2 copy.92
  315.3 10.1 %fusion.4 = f32[32,16,256]{2,1,0:T(8,128)S(1)} fusion(bf16[383,32,16]{0,2,1:T(8,128)(2,1)S(1)} %bitcast.104, f32[256,383,32]{1,0,2:T(8,128)} %reshape.183, pred[256,383]{1,0:T(8,128)(4,1)S(1)} %get-tuple-element.34, pred[256,383]{1,0:T(8,128)(4,1)S(1)} %get-tuple-element.33), kind=kOutput, calls=%fused_computation.6 | convolution fusion | flops 608681984 | bytes 13662720 | tf_op jit(solution)/shard_map/gts,sgc->tgc/dot_general | solution.py:47
  325.4 0.5 fusion.37
  325.9 0.1 fusion.36
  326.2 0.2 copy.97
  326.4 0.2 copy.98
  326.6 0.1 pad_maximum_fusion.7
  326.7 1.5 collective-permute-start.1
  328.2 182.5 %gather_fusion.1 = f32[99330,32]{1,0:T(8,128)} fusion(f32[32,128]{0,1:T(8,128)S(1)} %copy.94, s32[100352]{0:T(1024)S(1)} %pad_clamp_fusion), kind=kCustom, calls=%fused_computation.1 | custom fusion | bytes 25825800 | tf_op jit(solution)/shard_map/jit(_take)/gather | solution.py:40
  510.8 31.5 %copy.102 = f32[99330,32]{0,1:T(8,128)} copy(f32[99330,32]{1,0:T(8,128)} %gather_fusion.1) | data formatting | bytes 25428480 | tf_op jit(solution)/shard_map/jit(_take)/gather | solution.py:40
  542.3 30.9 %reshape.191 = f32[258,385,32]{1,0,2:T(8,128)} reshape(f32[99330,32]{0,1:T(8,128)} %copy.102) | data formatting | bytes 25428480 | tf_op jit(solution)/shard_map/jit(_take)/gather | solution.py:40
  573.1 0.4 fusion.33
  573.5 0.2 slice.196
  573.9 0.1 copy.99
  574.0 0.2 copy.111
  574.3 0.2 copy.112
  574.5 14.0 %fusion = f32[32,16,258]{2,1,0:T(8,128)S(1)} fusion(bf16[385,32,16]{0,2,1:T(8,128)(2,1)S(1)} %bitcast.101, f32[258,385,32]{1,0,2:T(8,128)} %reshape.191, pred[258,385]{1,0:T(8,128)(4,1)S(1)} %get-tuple-element.36, pred[258,385]{1,0:T(8,128)(4,1)S(1)} %get-tuple-element.35), kind=kOutput, calls=%fused_computation.2 | convolution fusion | flops 616640640 | bytes 13835524 | tf_op jit(solution)/shard_map/gts,sgc->tgc/dot_general | solution.py:47
  588.6 0.2 fusion.27
  588.8 0.3 pad_maximum_fusion
  589.0 1.2 add_convert_fusion.1
  590.3 13.3 %fusion.8 = bf16[256,8192]{1,0:T(8,128)(2,1)} fusion(bf16[256,3,512]{0,2,1:T(8,128)(2,1)S(1)} %add_convert_fusion.1, bf16[8192,3,512]{2,0,1:T(8,128)(2,1)} %param.8), kind=kOutput, calls=%fused_computation.15 | convolution fusion | flops 6444548096 | bytes 30146560 | tf_op jit(solution)/shard_map/dot_general | solution.py:113
  603.6 0.7 all-gather.5.cloned.1.call-update
  604.3 4.8 copy.116
  609.1 5.2 all-to-all-start
  614.4 0.8 copy.107
  615.2 85.0 %all-reduce.2.cloned.1.call-done = bf16[256,8192]{1,0:T(8,128)(2,1)} async-done(((bf16[256,8192]{1,0:T(8,128)(2,1)}), bf16[256,8192]{1,0:T(8,128)(2,1)}) %all-reduce.2.cloned.1.call-update) | async-done | bytes 4194320 | tf_op jit(solution)/shard_map/psum | solution.py:120
  700.2 3.3 convert_element_type.175
  703.5 0.1 copy-done.1
  703.6 1.3 copy-done.2
  704.9 1.7 fusion.16
  706.6 1.1 multiply_convert_fusion
  707.7 38.1 %all-gather.5.cloned.1.call-done = bf16[1024,1536]{0,1:T(8,128)(2,1)} async-done(((bf16[256,1536]{0,1:T(8,128)(2,1)}), bf16[1024,1536]{0,1:T(8,128)(2,1)}) %all-gather.5.cloned.1.call-update) | async-done | bytes 3145744 | tf_op jit(solution)/shard_map/all_gather | solution.py:131
  745.8 3.5 convolution_convert_fusion.3
  749.3 3.1 convolution_convert_fusion.2
  752.4 3.1 convolution_convert_fusion.1
  755.5 3.1 convolution_convert_fusion
  758.6 5.3 add_convert_fusion
  763.8 8.7 %copy.106 = bf16[2048,1536]{0,1:T(8,128)(2,1)} copy(bf16[2048,1536]{1,0:T(8,128)(2,1)} %add_convert_fusion) | data formatting | bytes 12582912 | tf_op jit(solution)/shard_map/convert_element_type | solution.py:143
  772.6 8.6 %copy.108 = bf16[2048,3,512]{2,0,1:T(8,128)(2,1)} copy(bf16[2048,3,512]{0,2,1:T(8,128)(2,1)} %bitcast.92) | data formatting | bytes 12582912
  (63 shorter events, 1.1 us)
Async XLA Ops:
  7.2 52.0 %all-gather.3.cloned.1.call-start = ((), (), s32[]{:S(2)}) async-start(), calls=%async_computation.1 | async-start | bytes 4718592 | tf_op jit(solution)/shard_map/all_gather | solution.py:53
  7.9 692.3 %all-reduce.2.cloned.1.call-start = ((), (), s32[]{:S(2)}) async-start(), calls=%async_computation.2 | async-start | bytes 8388608 | tf_op jit(solution)/shard_map/psum | solution.py:120
  22.6 39.9 %copy-start.6 = (f32[8192]{0:T(1024)}, f32[8192]{0:T(1024)S(1)}, u32[]{:S(2)}) copy-start(f32[8192]{0:T(1024)S(1)} %convert_element_type.145) | copy-start | bytes 98308
  22.6 34.8 %copy-start.9 = (f32[3,3,512]{2,1,0:T(4,128)S(1)}, f32[3,3,512]{2,1,0:T(4,128)}, u32[]{:S(2)}) copy-start(f32[3,3,512]{2,1,0:T(4,128)} %param.9) | copy-start | bytes 55300
  59.2 3.4 copy-start
  62.5 16.2 %copy-start.13 = (f32[256]{0:T(256)}, f32[256]{0:T(256)S(1)}, u32[]{:S(2)}) copy-start(f32[256]{0:T(256)S(1)} %fusion.13) | copy-start | bytes 3076
  62.7 16.0 %copy-start.11 = (f32[256]{0:T(256)}, f32[256]{0:T(256)S(1)}, u32[]{:S(2)}) copy-start(f32[256]{0:T(256)S(1)} %add_rsqrt_fusion) | copy-start | bytes 3076
  65.8 17.9 %copy-start.10 = (f32[32,128]{1,0:T(8,128)S(1)}, f32[32,128]{1,0:T(8,128)}, u32[]{:S(2)}) copy-start(f32[32,128]{1,0:T(8,128)} %param.10) | copy-start | bytes 49156
  79.7 233.3 %collective-permute-start = (bf16[130,1024]{1,0:T(8,128)(2,1)S(1)}, bf16[130,1024]{1,0:T(8,128)(2,1)S(1)}, u32[]{:S(2)}, u32[]{:S(2)}) collective-permute-start(bf16[130,1024]{1,0:T(8,128)(2,1)S(1)} %pad_maximum_fusion.5), channel_id=1, source_target_pairs={{0,8},{8,16},{16,24},{1,9},{9,17},{17,25},{2,10},{10,18},{18,26},{... | collective-permute-start | bytes 798728 | tf_op jit(solution)/shard_map/ppermute | solution.py:15
  294.5 18.2 %copy-start.8 = (bf16[256,512]{1,0:T(8,128)(2,1)S(1)}, bf16[256,512]{1,0:T(8,128)(2,1)}, u32[]{:S(2)}) copy-start(bf16[256,512]{1,0:T(8,128)(2,1)} %param.11) | copy-start | bytes 786436
  326.7 247.0 %collective-permute-start.1 = (bf16[135,512]{0,1:T(8,128)(2,1)S(1)}, bf16[135,512]{0,1:T(8,128)(2,1)S(1)}, u32[]{:S(2)}, u32[]{:S(2)}) collective-permute-start(bf16[135,512]{0,1:T(8,128)(2,1)S(1)} %pad_maximum_fusion.7), channel_id=1, source_target_pairs={{8,0},{16,8},{24,16},{9,1},{17,9},{25,17},{10,2},{18,10},{26,18},{... | collective-permute-start | bytes 414728 | tf_op jit(solution)/shard_map/ppermute | solution.py:15
  590.3 13.3 %copy-start.4 = (bf16[256,3,512]{0,2,1:T(8,128)(2,1)}, bf16[256,3,512]{0,2,1:T(8,128)(2,1)S(1)}, u32[]{:S(2)}) copy-start(bf16[256,3,512]{0,2,1:T(8,128)(2,1)S(1)} %add_convert_fusion.1) | copy-start | bytes 2359300
  603.6 142.2 %all-gather.5.cloned.1.call-start = ((), (), s32[]{:S(2)}) async-start(), calls=%async_computation.3 | async-start | bytes 3932160 | tf_op jit(solution)/shard_map/all_gather | solution.py:131
  609.1 5.2 copy-start.15
  609.1 98.6 %all-to-all-start = ((bf16[256,4,2048]{2,0,1:T(8,128)(2,1)}), bf16[256,4,2048]{2,0,1:T(8,128)(2,1)}, u32[]{:S(2)}, u32[]{:S(2)}) async-start(bf16[256,4,2048]{2,0,1:T(8,128)(2,1)} %bitcast.94), calls=%async_computation | async-start | bytes 8388608 | tf_op jit(solution)/shard_map/all_to_all | solution.py:128
  615.2 88.3 %copy-start.7 = (f32[8192]{0:T(1024)S(1)}, f32[8192]{0:T(1024)}, u32[]{:S(2)}) copy-start(f32[8192]{0:T(1024)} %copy-done.6) | copy-start | bytes 98308
  700.2 3.4 copy-start.1
  700.2 4.7 copy-start.2
  704.9 1.7 copy-start.14
  704.9 1.7 copy-start.5
  704.9 1.7 copy-start.12
  745.8 3.5 copy-start.3
Sparse Core Ops, SparseCore 0:
  9.6 49.5 all-gather.2
  603.7 96.4 all-reduce.1
  702.0 43.7 all-gather.4
where the time goes:
time: 797 us; the launch traced here: 788 us
  local copies, waits for them, and re-layouts  536 us (67%)
  waiting for transfers between devices  126 us (16%)
  matrix products  62.9 us (8%)
  other arithmetic  23.1 us (3%)
  blocking collectives  14.6 us (2%)
  between operations  14.6 us (2%)
  starting transfers between devices  10.6 us (1%)
    gather x6, local copies, waits for them, and re-layouts, band_matrix(): picked = jnp.take(tap_rows, jnp.clip(offsets, 0, LM - 1), axis=1)  474 us
    psum x1, waiting for transfers between devices, per_device(): lax.psum(partial_grad.astype(jnp.bfloat16), 'tp').astype(jnp.float32)  85 us
    unnamed x40, local copies, waits for them, and re-layouts  45.3 us
    all_gather x1, waiting for transfers between devices, per_device(): piece = lax.all_gather(grad_pre, 'seq', axis=0, tiled=True)  38.1 us
    dot_general x2, matrix products, grouped_apply(): jnp.einsum('gts,sgc->tgc', band, shaped, precision=lax.Precision.HIGHEST)  24.1 us
  transfers between devices with their start and end apart: 6, of which 3 were waited for; matrix products, arithmetic and copies ran while one was open for 66% of the time, Pallas kernels for 0%

commit v1 on v0

--- a/solution.py
+++ b/solution.py
@@ -7,6 +7,12 @@
 LS = 3
 LM = 128
 norm_eps = 1e-06
+
+
+def summed_here(x, axis):
+    blocks = lax.all_gather(x, axis, axis=0, tiled=False)
+    result = blocks.sum(axis=0)
+    return result
 
 
 def shifted(block, axis, distance):
@@ -117,7 +123,7 @@
     own_width = width // tp_count
     own_scaled = activations.astype(jnp.float32) * inv_rms
     own_gain = norm_gain.astype(jnp.float32)
-    whole_grad = lax.psum(partial_grad.astype(jnp.bfloat16), "tp").astype(jnp.float32)
+    whole_grad = summed_here(partial_grad.astype(jnp.bfloat16), "tp").astype(jnp.float32)
     stat = jnp.mean(gain_float * whole_grad * act_float, axis=1, keepdims=True) * inv_rms
     grad_slice = lax.dynamic_slice_in_dim(
         whole_grad, lax.axis_index("tp") * own_width, own_width, 1

time: 797 us -> 1000 us (1.25)
  waiting for transfers between devices: 126 us -> 313 us
  other arithmetic: 23.1 us -> 38.2 us
    all_gather x0 -> x1, waiting for transfers between devices: none -> 248 us  [summed_here(): blocks = lax.all_gather(x, axis, axis=0, tiled=False)]
    psum x1 -> x0, waiting for transfers between devices: 85 us -> none  [per_device(): lax.psum(partial_grad.astype(jnp.bfloat16), 'tp').astype(jnp.float32)]
    all_to_all x1, waiting for transfers between devices: 0.01 us -> 61.9 us  [per_device(): lax.all_to_all(normed, 'seq', split_axis=1, concat_axis=0, tiled=True)]
    all_gather x1, waiting for transfers between devices: 38.1 us -> 0.01 us  [per_device(): piece = lax.all_gather(grad_pre, 'seq', axis=0, tiled=True)]
    reduce_sum x0 -> x1, other arithmetic: none -> 14.3 us  [summed_here(): result = blocks.sum(axis=0)]
    unnamed x40 -> x38, local copies, waits for them, and re-layouts: 45.3 us -> 44.2 us
  transfers between devices with their start and end apart: 6 -> 6, of which waited for: 3 -> 3; matrix products, arithmetic and copies ran while one was open for 66% -> 57% of each run, Pallas kernels for 0% -> 0%
where the time goes in v1:
time: 1000 us; the launch traced here: 993 us
  local copies, waits for them, and re-layouts  538 us (54%)
  waiting for transfers between devices  313 us (31%)
  matrix products  64.1 us (6%)
  other arithmetic  38.2 us (4%)
  blocking collectives  14.6 us (1%)
  between operations  14.4 us (1%)
  starting transfers between devices  10.7 us (1%)
    gather x6, local copies, waits for them, and re-layouts, band_matrix(): picked = jnp.take(tap_rows, jnp.clip(offsets, 0, LM - 1), axis=1)  475 us
    all_gather x1, waiting for transfers between devices, summed_here(): blocks = lax.all_gather(x, axis, axis=0, tiled=False)  248 us
    all_to_all x1, waiting for transfers between devices, per_device(): lax.all_to_all(normed, 'seq', split_axis=1, concat_axis=0, tiled=True)  61.9 us
    unnamed x38, local copies, waits for them, and re-layouts  44.2 us
    dot_general x2, matrix products, grouped_apply(): jnp.einsum('gts,sgc->tgc', band, shaped, precision=lax.Precision.HIGHEST)  24.1 us
  transfers between devices with their start and end apart: 6, of which 3 were waited for; matrix products, arithmetic and copies ran while one was open for 57% of the time, Pallas kernels for 0%

profile of v1, /device:TPU:0, one launch (start us, length us, event | category | flops | bytes accessed | tf_op | source)
XLA Modules:
  0.0 993.2 jit_solution(52375864635151756)
XLA Ops:
  7.2 0.7 all-gather.5.cloned.1.call-update
  7.9 14.6 %all_gather.16 = bf16[8192]{0:T(1024)(128)(2,1)S(1)} all-gather(bf16[1024]{0:T(1024)(128)(2,1)} %param.7), channel_id=1, replica_groups=mesh['seq'=4,'tp'=8] {'tp'}, dimensions={0}, use_global_device_ids=true | all-gather | bytes 18432 | tf_op jit(solution)/shard_map/all_gather | solution.py:60
  22.6 32.5 %copy.97 = bf16[8192,3,512]{0,2,1:T(8,128)(2,1)} copy(bf16[8192,3,512]{2,0,1:T(8,128)(2,1)} %param.8) | data formatting | bytes 50331648 | tf_op args[2]
  55.1 0.5 reshape.180
  55.6 0.2 compare_select_fusion
  55.8 0.5 reshape.188
  56.4 2.8 all-gather.5.cloned.1.call-done
  59.2 3.3 fusion.13
  62.5 0.2 copy-done.1
  62.7 3.2 fusion.15
  65.9 12.8 %convolution_convert_fusion.4 = bf16[256,1536]{1,0:T(8,128)(2,1)S(1)} fusion(bf16[256,8192]{1,0:T(8,128)(2,1)} %fusion.15, bf16[8192,1536]{0,1:T(8,128)(2,1)} %bitcast.94), kind=kOutput, calls=%fused_computation.32 | convolution fusion | flops 6442844160 | bytes 30146560 | tf_op jit(solution)/shard_map/dot_general | solution.py:73
  78.7 0.3 copy.98
  79.0 0.2 slice.177
  79.3 0.2 copy.100
  79.5 0.1 copy.99
  79.7 3.6 collective-permute-start
  83.2 0.2 fusion.43
  83.5 180.3 %gather_fusion = f32[98048,32]{1,0:T(8,128)} fusion(f32[32,128]{0,1:T(8,128)S(1)} %copy.103, s32[98304]{0:T(1024)S(1)} %pad_clamp_fusion.1), kind=kCustom, calls=%fused_computation | custom fusion | bytes 25492480 | tf_op jit(solution)/shard_map/jit(_take)/gather | solution.py:46
  263.8 31.0 %copy.104 = f32[98048,32]{0,1:T(8,128)} copy(f32[98048,32]{1,0:T(8,128)} %gather_fusion) | data formatting | bytes 25100288 | tf_op jit(solution)/shard_map/jit(_take)/gather | solution.py:46
  294.8 18.2 %reshape.183 = f32[256,383,32]{1,0,2:T(8,128)} reshape(f32[98048,32]{0,1:T(8,128)} %copy.104) | data formatting | bytes 25100288 | tf_op jit(solution)/shard_map/jit(_take)/gather | solution.py:46
  313.1 0.1 copy.105
  313.3 0.2 copy.123
  313.5 1.7 add_convert_fusion.2
  315.3 0.1 slice.192
  315.5 0.2 copy.101
  315.7 10.1 %fusion.4 = f32[32,16,256]{2,1,0:T(8,128)S(1)} fusion(bf16[383,32,16]{0,2,1:T(8,128)(2,1)S(1)} %bitcast.106, f32[256,383,32]{1,0,2:T(8,128)} %reshape.183, pred[256,383]{1,0:T(8,128)(4,1)S(1)} %get-tuple-element.34, pred[256,383]{1,0:T(8,128)(4,1)S(1)} %get-tuple-element.33), kind=kOutput, calls=%fused_computation.6 | convolution fusion | flops 608681984 | bytes 13662720 | tf_op jit(solution)/shard_map/gts,sgc->tgc/dot_general | solution.py:53
  325.8 0.5 fusion.37
  326.3 0.1 fusion.36
  326.5 0.2 copy.106
  326.8 0.2 copy.107
  327.0 0.1 pad_maximum_fusion.7
  327.1 1.5 collective-permute-start.1
  328.6 183.2 %gather_fusion.1 = f32[99330,32]{1,0:T(8,128)} fusion(f32[32,128]{0,1:T(8,128)S(1)} %copy.103, s32[100352]{0:T(1024)S(1)} %pad_clamp_fusion), kind=kCustom, calls=%fused_computation.1 | custom fusion | bytes 25825800 | tf_op jit(solution)/shard_map/jit(_take)/gather | solution.py:46
  511.8 31.5 %copy.111 = f32[99330,32]{0,1:T(8,128)} copy(f32[99330,32]{1,0:T(8,128)} %gather_fusion.1) | data formatting | bytes 25428480 | tf_op jit(solution)/shard_map/jit(_take)/gather | solution.py:46
  543.3 30.9 %reshape.191 = f32[258,385,32]{1,0,2:T(8,128)} reshape(f32[99330,32]{0,1:T(8,128)} %copy.111) | data formatting | bytes 25428480 | tf_op jit(solution)/shard_map/jit(_take)/gather | solution.py:46
  574.2 0.4 fusion.33
  574.5 0.2 slice.196
  574.9 0.1 copy.108
  575.1 0.2 copy.124
  575.4 0.2 copy.125
  575.6 14.0 %fusion = f32[32,16,258]{2,1,0:T(8,128)S(1)} fusion(bf16[385,32,16]{0,2,1:T(8,128)(2,1)S(1)} %bitcast.103, f32[258,385,32]{1,0,2:T(8,128)} %reshape.191, pred[258,385]{1,0:T(8,128)(4,1)S(1)} %get-tuple-element.36, pred[258,385]{1,0:T(8,128)(4,1)S(1)} %get-tuple-element.35), kind=kOutput, calls=%fused_computation.2 | convolution fusion | flops 616640640 | bytes 13835524 | tf_op jit(solution)/shard_map/gts,sgc->tgc/dot_general | solution.py:53
  589.6 0.2 fusion.27
  589.8 0.3 pad_maximum_fusion
  590.0 2.0 add_convert_fusion.1
  592.1 0.4 all-gather.9.cloned.1.call-start
  592.5 13.9 %fusion.8 = bf16[256,8192]{1,0:T(8,128)(2,1)} fusion(bf16[256,3,512]{0,2,1:T(8,128)(2,1)} %add_convert_fusion.1, bf16[8192,3,512]{2,0,1:T(8,128)(2,1)} %param.8), kind=kOutput, calls=%fused_computation.15 | convolution fusion | flops 6444548096 | bytes 30146560 | tf_op jit(solution)/shard_map/dot_general | solution.py:119
  606.4 6.4 copy.114
  612.8 5.1 all-to-all-start
  618.0 0.8 copy.120
  618.8 61.9 %all-to-all-done = bf16[256,4,2048]{0,2,1:T(8,128)(2,1)} async-done(((bf16[256,4,2048]{0,2,1:T(8,128)(2,1)}), bf16[256,4,2048]{0,2,1:T(8,128)(2,1)}, u32[]{:S(2)}, u32[]{:S(2)}) %all-to-all-start) | async-done | bytes 4194336 | tf_op jit(solution)/shard_map/all_to_all | solution.py:134
  680.7 3.4 convolution_convert_fusion.3
  684.2 3.2 convolution_convert_fusion.2
  687.4 3.3 convolution_convert_fusion.1
  690.7 3.4 convolution_convert_fusion
  694.1 5.3 add_convert_fusion
  699.4 8.8 copy.119
  708.2 8.6 copy.121
  716.8 247.9 %all-gather.9.cloned.1.call-done = bf16[2048,8192]{1,0:T(8,128)(2,1)} async-done(((bf16[256,8192]{1,0:T(8,128)(2,1)}), bf16[2048,8192]{1,0:T(8,128)(2,1)}) %all-gather.9.cloned.1.call-update) | async-done | bytes 33554448 | tf_op jit(solution)/shard_map/all_gather | solution.py:13
  964.7 14.3 %reduce_sum.31 = bf16[256,8192]{1,0:T(8,128)(2,1)} reduce(bf16[8,256,8192]{2,1,0:T(8,128)(2,1)} %bitcast.93, bf16[]{:T(256)} %constant.30.clone.1), dimensions={0}, to_apply=%region_1.2 | reduce | flops 14680064 | bytes 37748736 | tf_op jit(solution)/shard_map/reduce_sum | solution.py:14
  979.0 3.3 convert_element_type.177
  982.4 0.1 copy-done
  982.5 1.3 copy-done.2
  983.8 1.6 fusion.16
  985.4 1.1 multiply_convert_fusion
  (62 shorter events, 1.2 us)
Async XLA Ops:
  7.2 52.0 %all-gather.5.cloned.1.call-start = ((), (), s32[]{:S(2)}) async-start(), calls=%async_computation.1 | async-start | bytes 4718592 | tf_op jit(solution)/shard_map/all_gather | solution.py:59
  7.9 672.8 %all-gather.7.cloned.1.call-start = ((), (), s32[]{:S(2)}) async-start(), calls=%async_computation.2 | async-start | bytes 3932160 | tf_op jit(solution)/shard_map/all_gather | solution.py:137
  22.6 39.9 %copy-start.5 = (f32[8192]{0:T(1024)}, f32[8192]{0:T(1024)S(1)}, u32[]{:S(2)}) copy-start(f32[8192]{0:T(1024)S(1)} %convert_element_type.147) | copy-start | bytes 98308
  22.6 33.7 %copy-start.8 = (f32[3,3,512]{2,1,0:T(4,128)S(1)}, f32[3,3,512]{2,1,0:T(4,128)}, u32[]{:S(2)}) copy-start(f32[3,3,512]{2,1,0:T(4,128)} %param.9) | copy-start | bytes 55300
  59.2 3.4 copy-start.1
  62.5 16.2 %copy-start.12 = (f32[256]{0:T(256)}, f32[256]{0:T(256)S(1)}, u32[]{:S(2)}) copy-start(f32[256]{0:T(256)S(1)} %fusion.13) | copy-start | bytes 3076
  62.7 16.0 %copy-start.10 = (f32[256]{0:T(256)}, f32[256]{0:T(256)S(1)}, u32[]{:S(2)}) copy-start(f32[256]{0:T(256)S(1)} %add_rsqrt_fusion) | copy-start | bytes 3076
  65.8 17.6 %copy-start.9 = (f32[32,128]{1,0:T(8,128)S(1)}, f32[32,128]{1,0:T(8,128)}, u32[]{:S(2)}) copy-start(f32[32,128]{1,0:T(8,128)} %param.10) | copy-start | bytes 49156
  79.7 233.6 %collective-permute-start = (bf16[130,1024]{1,0:T(8,128)(2,1)S(1)}, bf16[130,1024]{1,0:T(8,128)(2,1)S(1)}, u32[]{:S(2)}, u32[]{:S(2)}) collective-permute-start(bf16[130,1024]{1,0:T(8,128)(2,1)S(1)} %pad_maximum_fusion.5), channel_id=1, source_target_pairs={{0,8},{8,16},{16,24},{1,9},{9,17},{17,25},{2,10},{10,18},{18,26},{... | collective-permute-start | bytes 798728 | tf_op jit(solution)/shard_map/ppermute | solution.py:21
  294.8 18.2 %copy-start.7 = (bf16[256,512]{1,0:T(8,128)(2,1)S(1)}, bf16[256,512]{1,0:T(8,128)(2,1)}, u32[]{:S(2)}) copy-start(bf16[256,512]{1,0:T(8,128)(2,1)} %param.11) | copy-start | bytes 786436
  327.1 247.7 %collective-permute-start.1 = (bf16[135,512]{0,1:T(8,128)(2,1)S(1)}, bf16[135,512]{0,1:T(8,128)(2,1)S(1)}, u32[]{:S(2)}, u32[]{:S(2)}) collective-permute-start(bf16[135,512]{0,1:T(8,128)(2,1)S(1)} %pad_maximum_fusion.7), channel_id=1, source_target_pairs={{8,0},{16,8},{24,16},{9,1},{17,9},{25,17},{10,2},{18,10},{26,18},{... | collective-permute-start | bytes 414728 | tf_op jit(solution)/shard_map/ppermute | solution.py:21
  592.1 372.6 %all-gather.9.cloned.1.call-start = ((), (), s32[]{:S(2)}) async-start(), calls=%async_computation.3 | async-start | bytes 37748736 | tf_op jit(solution)/shard_map/all_gather | solution.py:13
  612.8 5.1 copy-start.14
  612.8 67.9 %all-to-all-start = ((bf16[256,4,2048]{0,2,1:T(8,128)(2,1)}), bf16[256,4,2048]{0,2,1:T(8,128)(2,1)}, u32[]{:S(2)}, u32[]{:S(2)}) async-start(bf16[256,4,2048]{0,2,1:T(8,128)(2,1)} %bitcast.96), calls=%async_computation | async-start | bytes 8388608 | tf_op jit(solution)/shard_map/all_to_all | solution.py:134
  680.7 3.4 copy-start.3
  979.0 3.4 copy-start
  979.0 4.7 copy-start.2
  979.0 4.7 copy-start.6
  983.8 1.6 copy-start.13
  983.8 1.6 copy-start.4
  983.8 1.6 copy-start.11
Sparse Core Ops, SparseCore 0:
  9.6 49.5 all-gather.4
  592.2 79.5 all-gather.6
  673.4 291.1 all-gather.8
